TPU v7x, 32 devices: a whole 2x2x4 slice. The times are simulated.
32 devices in a mesh: cell: 8 (over y, x, core), view: 4 (over z).
Axes of the slice: x: 2, y: 2, z: 4, core: 2. Of those that a mesh axis runs over, the one named last changes fastest.
Arguments:
- attributes: float32 [14, 65536], P(None, ('cell', 'view'))
- tile_anchor: float32 [2, 1536], P(None, ('cell', 'view')), may hold values from -2 to 4
- target: float32 [1536, 4, 256], P(('cell', 'view'))
- preconditioner: float32 [14, 14, 65536], P(None, None, ('cell', 'view')), as said below
- send_index: int32 [32, 32, 96], P(('cell', 'view')), may hold values from 0 to 2047, as said below
- tile_list: int32 [1536, 64], P(('cell', 'view')), may hold values from 0 to 3071, as said below
- pair_index: int32 [1536], P(('cell', 'view')), may hold values from 0 to 47, as said below
Outputs:
- update: float32 [14, 65536], P(None, ('cell', 'view'))
- step_residual: float32 [14, 65536], P(None, ('cell', 'view'))
Inputs may be any that keep to these rules, and one draw needn't show every extreme that they name: `send_index`: for each pair of devices, the 96 local Gaussian numbers that one sends to the other are distinct. `tile_list`: entries number a device's received rows by source device, then slot (96 a source); on each device the entries of its tiles are a permutation of those row numbers. `pair_index`: on each device, a permutation of its tiles' local numbers. `preconditioner`: each 14 x 14 block is symmetric and diagonally dominant with a positive diagonal.
All inputs are finite; a program needn't handle non-finite values.
Results may differ from a plain program's by a relative error of at most 0.0003.
Values sent between devices are 32-bit elements; how exact they have to be, the bound alone decides.
No kernel may reach another device: no remote copies, remote signals or barrier semaphores. Data moves between devices by JAX's collectives and lax.ppermute only.
A program may use at most 128 MiB of HBM per device.

v0:
```python
import math
import jax
import jax.numpy as jnp
from jax import lax
from jax.sharding import PartitionSpec as P

ITERS = 2
DAMPING = 0.5
PRIOR_WEIGHT = 0.3
DILATION = 0.3


def shifted(value, axis, by):
    devices = lax.axis_size(axis)
    return lax.ppermute(value, axis, [(i, (i + by) % devices) for i in range(devices)])


def camera_axes():
    tilt_cos, tilt_sin = (math.cos(0.3), math.sin(0.3))
    turn_cos, turn_sin = (math.cos(0.2), math.sin(0.2))
    return (
        (turn_cos, turn_sin * tilt_sin, turn_sin * tilt_cos),
        (0.0, tilt_cos, -tilt_sin),
        (-turn_sin, turn_cos * tilt_sin, turn_cos * tilt_cos),
    )


def render(listed, anchor):
    camera = camera_axes()
    factor_rows = (
        (jnp.exp(listed[3]), None, None),
        (listed[4], jnp.exp(listed[5]), None),
        (listed[6], listed[7], jnp.exp(listed[8])),
    )
    screen = []
    for axis_row in range(2):
        place_value = (
            camera[axis_row][0] * listed[0]
            + camera[axis_row][1] * listed[1]
            + camera[axis_row][2] * listed[2]
        )
        screen.append(place_value - anchor[axis_row][:, None])
    depth_values = camera[2][0] * listed[0] + camera[2][1] * listed[1] + camera[2][2] * listed[2]
    projected = []
    for axis_row in range(2):
        row_terms = []
        for column_index in range(3):
            total_term = camera[axis_row][column_index] * factor_rows[column_index][column_index]
            for inner_index in range(column_index + 1, 3):
                total_term = (
                    total_term
                    + camera[axis_row][inner_index] * factor_rows[inner_index][column_index]
                )
            row_terms.append(total_term)
        projected.append(row_terms)
    cov_xx = (
        projected[0][0] * projected[0][0]
        + projected[0][1] * projected[0][1]
        + projected[0][2] * projected[0][2]
        + DILATION
    )
    cov_xy = (
        projected[0][0] * projected[1][0]
        + projected[0][1] * projected[1][1]
        + projected[0][2] * projected[1][2]
    )
    cov_yy = (
        projected[1][0] * projected[1][0]
        + projected[1][1] * projected[1][1]
        + projected[1][2] * projected[1][2]
        + DILATION
    )
    determinant = cov_xx * cov_yy - cov_xy * cov_xy
    conic_xx = (cov_yy / determinant)[..., None]
    conic_xy = (-cov_xy / determinant)[..., None]
    conic_yy = (cov_xx / determinant)[..., None]
    opacity = 0.99 * jax.nn.sigmoid(listed[9])
    pixels = jnp.arange(256)
    pixel_x = (pixels % 16).astype(jnp.float32) + 0.5
    pixel_y = (pixels // 16).astype(jnp.float32) + 0.5
    offset_x = pixel_x - screen[0][:, :, None]
    offset_y = pixel_y - screen[1][:, :, None]
    exponent = -0.5 * (
        conic_xx * offset_x * offset_x
        + 2.0 * conic_xy * offset_x * offset_y
        + conic_yy * offset_y * offset_y
    )
    coverage = opacity[..., None] * jnp.exp(exponent)
    log_keep = jnp.log1p(-coverage)
    earlier = (jnp.arange(64)[None, :] < jnp.arange(64)[:, None]).astype(jnp.float32)
    before = jnp.einsum("jk,bkp->bjp", earlier, log_keep, precision=lax.Precision.HIGHEST)
    weight = jnp.exp(before) * coverage
    colours = jnp.einsum("cbk,bkp->bcp", listed[10:14], weight, precision=lax.Precision.HIGHEST)
    depths = jnp.einsum("bk,bkp->bp", depth_values, weight, precision=lax.Precision.HIGHEST)
    return (colours, depths)


def local(attributes, tile_anchor, target, preconditioner, send_index, tile_list, pair_index):
    cell_count = lax.axis_size("cell")
    view_count = lax.axis_size("view")
    devices = cell_count * view_count
    send_ids = send_index[0]
    slot_count = send_ids.shape[1]
    tiles_here = tile_list.shape[0]
    entries = tile_list.reshape(-1)
    entry_inverse = jnp.argsort(entries)
    pair_inverse = jnp.argsort(pair_index)

    def route(outgoing, forward):
        if forward:
            return lax.all_to_all(
                outgoing, ("cell", "view"), split_axis=1, concat_axis=1, tiled=True
            )
        return lax.all_to_all(outgoing, ("cell", "view"), split_axis=1, concat_axis=1, tiled=True)

    def deliver(values):
        received = route(values[:, send_ids], True)
        return received.reshape(14, -1)[:, entries].reshape(14, tiles_here, 64)

    def collect(cotangent):
        flattened = cotangent.reshape(14, -1)[:, entry_inverse].reshape(14, devices, slot_count)
        returned = route(flattened, False)
        summed = jax.ops.segment_sum(
            returned.reshape(14, -1).T, send_ids.reshape(-1), num_segments=attributes.shape[1]
        )
        return summed.T

    def neighbour(depth_map):
        return shifted(depth_map, "view", -1)[pair_index]

    def depth_cotangent(prior_term):
        arrived = shifted(prior_term[pair_inverse], "view", 1)
        return PRIOR_WEIGHT * prior_term - PRIOR_WEIGHT * arrived

    def apply_scaling(vector):
        return jnp.einsum("ijg,jg->ig", preconditioner, vector, precision=lax.Precision.HIGHEST)

    def global_inner(first, second):
        return lax.psum(jnp.sum(first * second), ("cell", "view"))

    def local_render(values):
        return render(values, tile_anchor)

    listed_now = deliver(attributes)
    (colours, depths), pull_fn = jax.vjp(local_render, listed_now)
    _, tangent_fn = jax.vjp(pull_fn, (jnp.zeros_like(colours), jnp.zeros_like(depths)))
    photometric = colours - target
    prior_term = PRIOR_WEIGHT * (depths - neighbour(depths))
    gradient = collect(pull_fn((photometric, depth_cotangent(prior_term)))[0])
    residual = -gradient
    solution = jnp.zeros_like(attributes)
    scaled = apply_scaling(residual)
    direction = scaled
    scaled_norm = global_inner(residual, scaled)
    for iteration in range(ITERS):
        colour_tangent, depth_tangent = tangent_fn((deliver(direction),))[0]
        prior_tangent = PRIOR_WEIGHT * (depth_tangent - neighbour(depth_tangent))
        normal_image = (
            collect(pull_fn((colour_tangent, depth_cotangent(prior_tangent)))[0])
            + DAMPING * direction
        )
        curvature_sum = lax.psum(jnp.sum(direction * normal_image), ("cell", "view"))
        step_size = scaled_norm / curvature_sum
        solution = solution + step_size * direction
        residual = residual - step_size * normal_image
        if iteration + 1 < ITERS:
            scaled = apply_scaling(residual)
            next_norm = global_inner(residual, scaled)
            direction = scaled + next_norm / scaled_norm * direction
            scaled_norm = next_norm
    return (solution, residual)


def solution(mesh):
    in_specs = (
        P(None, ("cell", "view")),
        P(None, ("cell", "view")),
        P(("cell", "view"), None, None),
        P(None, None, ("cell", "view")),
        P(("cell", "view"), None, None),
        P(("cell", "view"), None),
        P(("cell", "view")),
    )
    out_specs = (P(None, ("cell", "view")), P(None, ("cell", "view")))
    return jax.shard_map(local, mesh=mesh, in_specs=in_specs, out_specs=out_specs, check_vma=False)
```

profile of v0, /device:TPU:0, one launch (start us, length us, event | category | flops | bytes accessed | tf_op | source)
XLA Modules:
  0.0 688.7 jit_solution(14497731297453291714)
XLA Ops:
  2.7 8.1 %gather_fusion = f32[3072,14]{1,0:T(8,128)S(1)} fusion(f32[14,2048]{0,1:T(8,128)S(1)} %copy.404, s32[3072]{0:T(1024)S(1)} %broadcast_clamp_fusion.1), kind=kCustom, calls=%fused_computation | custom fusion | bytes 356352 | tf_op jit(solution)/shard_map/gather | solution.py:117
  12.1 7.3 %all-to-all-start = ((f32[14,32,96]{2,0,1:T(8,128)}), f32[14,32,96]{2,0,1:T(8,128)S(1)}, u32[]{:S(2)}, u32[]{:S(2)}) async-start(f32[14,32,96]{2,0,1:T(8,128)} %bitcast.2), calls=%async_computation | async-start | bytes 524288 | tf_op jit(solution)/shard_map/all_to_all | solution.py:111
  22.8 5.8 sort.35
  30.3 8.1 %gather_fusion.1 = f32[3072,14]{1,0:T(8,128)S(1)} fusion(f32[14,3072]{0,1:T(8,128)S(1)} %bitcast.428, s32[3072]{0:T(1024)S(1)} %broadcast_clamp_fusion), kind=kCustom, calls=%fused_computation.1 | custom fusion | bytes 356352 | tf_op jit(solution)/shard_map/gather | solution.py:118
  45.7 10.2 %bitcast_multiply_fusion.8 = (f32[48,64,256]{2,1,0:T(8,128)S(1)}, f32[48,256,64]{1,2,0:T(8,128)}) fusion(f32[48,64]{1,0:T(8,128)S(1)} %get-tuple-element.224, f32[48,64]{1,0:T(8,128)S(1)} %broadcast_subtract_fusion, f32[256]{0:T(256)S(1)} %copy-done.163, f32[48,64]{1,0:T(8,128)S(1)} %get-tuple-element.223, f32[48,64]{1,0:T(8,128)S(1)} %broadcast_subtract_fusion.1, ...), kind=kOutput, calls=%fused_computation.206 | convolution fusion | flops 624431104 | bytes 6367232 | tf_op jit(solution)/shard_map/jvp(jk,bkp->bjp)/dot_general | solution.py:91
  70.2 4.3 fusion.234
  89.8 13.4 %fusion.44 = (f32[48,64]{1,0:T(8,128)S(1)}, f32[48,64]{1,0:T(8,128)S(1)}, f32[48,64]{1,0:T(8,128)S(1)}, f32[48,64]{1,0:T(8,128)S(1)}, f32[48,64]{1,0:T(8,128)S(1)}, /*index=5*/f32[48,64]{1,0:T(8,128)S(1)}) fusion(f32[48,64]{1,0:T(8,128)S(1)} %copy-done.81, f32[48,64]{1,0:T(8,128)S(1)} %copy-done.142, f32[256]{0:T(256)S(1)} %copy-done.164, ...), kind=kOutput, calls=%fused_computation.113 | convolution fusion | flops 651937792 | bytes 6502400 | tf_op jit(solution)/shard_map/transpose(jvp(jk,bkp->bjp))/dot_general | solution.py:91
  107.0 13.2 %gather_fusion.4 = f32[3072,14]{1,0:T(8,128)} fusion(f32[14,3072]{0,1:T(8,128)} %bitcast.431, s32[3072]{0:T(1024)} %fusion.294), kind=kCustom, calls=%fused_computation.4 | custom fusion | bytes 356352 | tf_op jit(solution)/shard_map/gather | solution.py:121
  122.9 6.2 all-to-all-start.1
  129.8 12.3 %copy.448 = f32[14,14,2048]{0,1,2:T(8,128)} copy(f32[14,14,2048]{2,1,0:T(8,128)} %param.10) | data formatting | bytes 3211264 | tf_op args[3]
  146.5 18.4 %scatter_custom_fusion = f32[2048,14]{1,0:T(8,128)} fusion(s32[3072]{0:T(1024)} %reshape.2786, f32[3072,14]{1,0:T(8,128)} %copy.415, f32[]{:T(128)} %constant.25.clone.1), kind=kCustom, calls=%fused_computation.298 | custom fusion | flops 43008 | bytes 115200 | tf_op jit(solution)/shard_map/scatter-add | solution.py:123
  166.2 17.7 %fusion.338 = f32[2048,1,14]{2,1,0:T(1,128)} fusion(f32[14,2048,1]{0,2,1:T(1,128)S(1)} %bitcast.433, f32[14,14,2048]{0,1,2:T(8,128)} %copy.448), kind=kOutput, calls=%fused_computation.628 | convolution fusion | flops 4816896 | bytes 1835008 | tf_op jit(solution)/shard_map/ijg,jg->ig/dot_general | solution.py:136
  183.9 12.0 %gather_fusion.5 = f32[3072,14]{1,0:T(8,128)} fusion(f32[14,2048]{0,1:T(8,128)} %bitcast.419, s32[3072]{0:T(1024)S(1)} %broadcast_clamp_fusion.1), kind=kCustom, calls=%fused_computation.5 | custom fusion | bytes 356352 | tf_op jit(solution)/shard_map/gather | solution.py:117
  198.6 16.1 %all_to_all.30 = f32[14,32,96]{2,0,1:T(8,128)} all-to-all(f32[14,32,96]{2,0,1:T(8,128)} %bitcast.447), channel_id=1, replica_groups=mesh['cell'=8,'view'=4] {'cell','view'}, dimensions={1} | all-to-all | bytes 344064 | tf_op jit(solution)/shard_map/all_to_all | solution.py:111
  217.3 12.2 %gather_fusion.6 = f32[3072,14]{1,0:T(8,128)} fusion(f32[14,3072]{0,1:T(8,128)} %bitcast.429, s32[3072]{0:T(1024)S(1)} %copy-done.90), kind=kCustom, calls=%fused_computation.6 | custom fusion | bytes 356352 | tf_op jit(solution)/shard_map/gather | solution.py:118
  256.2 14.3 %fusion.53 = f32[48,64,256]{2,1,0:T(8,128)S(1)} fusion(f32[48,256,64]{1,2,0:T(8,128)S(1)} %copy-done.174, f32[48,64]{1,0:T(8,128)S(1)} %copy-done.158, f32[48,64]{1,0:T(8,128)S(1)} %get-tuple-element.189, f32[48,64]{1,0:T(8,128)S(1)} %neg.806, f32[48,64]{1,0:T(8,128)S(1)} %copy-done.160, f32[48,64]{1,0:T(8,128)S(1)} %get-tuple-element.188, ...), kind=kOutput, calls=%fused_computation.122 | convolution fusion | flops 663752704 | bytes 6477824 | tf_op jit(solution)/shard_map/transpose(jvp(transpose(jvp(jk,bkp->bjp))))/dot_general | solution.py:91
  293.3 13.3 %fusion.55 = (f32[48,64]{1,0:T(8,128)S(1)}, f32[48,64]{1,0:T(8,128)S(1)}, f32[48,64]{1,0:T(8,128)S(1)}, f32[48,64]{1,0:T(8,128)S(1)}, f32[48,64]{1,0:T(8,128)S(1)}, /*index=5*/f32[48,64]{1,0:T(8,128)S(1)}) fusion(f32[48,64]{1,0:T(8,128)S(1)} %copy-done.83, f32[48,64]{1,0:T(8,128)S(1)} %copy-done.144, f32[256]{0:T(256)S(1)} %copy-done.166, ...), kind=kOutput, calls=%fused_computation.124 | convolution fusion | flops 651937792 | bytes 6502400 | tf_op jit(solution)/shard_map/transpose(jvp(jk,bkp->bjp))/dot_general | solution.py:91
  313.2 13.2 %gather_fusion.9 = f32[3072,14]{1,0:T(8,128)} fusion(f32[14,3072]{0,1:T(8,128)} %bitcast.432, s32[3072]{0:T(1024)} %fusion.294), kind=kCustom, calls=%fused_computation.9 | custom fusion | bytes 356352 | tf_op jit(solution)/shard_map/gather | solution.py:121
  329.0 12.8 %all_to_all.31 = f32[14,32,96]{2,0,1:T(8,128)S(1)} all-to-all(f32[14,32,96]{2,0,1:T(8,128)} %copy.425), channel_id=1, replica_groups=mesh['cell'=8,'view'=4] {'cell','view'}, dimensions={1} | all-to-all | bytes 344064 | tf_op jit(solution)/shard_map/all_to_all | solution.py:114
  345.3 18.3 %scatter_custom_fusion.1 = f32[2048,14]{1,0:T(8,128)} fusion(s32[3072]{0:T(1024)} %reshape.2786, f32[3072,14]{1,0:T(8,128)} %copy.427, f32[]{:T(128)} %constant.25.clone.1), kind=kCustom, calls=%fused_computation.296 | custom fusion | flops 43008 | bytes 115200 | tf_op jit(solution)/shard_map/scatter-add | solution.py:123
  366.4 38.6 %all-reduce.51 = (f32[]{:T(128)}, f32[]{:T(128)}) all-reduce(f32[]{:T(128)} %get-tuple-element.35, f32[]{:T(128)} %get-tuple-element.34), channel_id=1, replica_groups=mesh['cell'=8,'view'=4] {'cell','view'}, use_global_device_ids=true, to_apply=%region_10.11 | all-reduce | flops 2 | bytes 16 | tf_op jit(solution)/shard_map/psum | solution.py:139
  408.3 17.4 %fusion.342 = f32[2048,1,14]{2,1,0:T(1,128)S(1)} fusion(f32[14,2048,1]{0,2,1:T(1,128)S(1)} %bitcast.424, f32[14,14,2048]{0,1,2:T(8,128)} %copy.448), kind=kOutput, calls=%fused_computation.632 | convolution fusion | flops 4816896 | bytes 1835008 | tf_op jit(solution)/shard_map/ijg,jg->ig/dot_general | solution.py:136
  427.7 40.6 %psum.30 = f32[]{:T(128)} all-reduce(f32[]{:T(128)} %multiply_reduce_fusion.4), channel_id=1, replica_groups=mesh['cell'=8,'view'=4] {'cell','view'}, use_global_device_ids=true, to_apply=%region_21.22 | all-reduce | flops 1 | bytes 8 | tf_op jit(solution)/shard_map/psum | solution.py:139
  472.2 12.1 %gather_fusion.10 = f32[3072,14]{1,0:T(8,128)} fusion(f32[14,2048]{0,1:T(8,128)} %multiply_add_fusion.7, s32[3072]{0:T(1024)S(1)} %broadcast_clamp_fusion.1), kind=kCustom, calls=%fused_computation.10 | custom fusion | bytes 356352 | tf_op jit(solution)/shard_map/gather | solution.py:117
  486.9 14.7 %all_to_all.32 = f32[14,32,96]{2,0,1:T(8,128)} all-to-all(f32[14,32,96]{2,0,1:T(8,128)} %bitcast.448), channel_id=1, replica_groups=mesh['cell'=8,'view'=4] {'cell','view'}, dimensions={1} | all-to-all | bytes 344064 | tf_op jit(solution)/shard_map/all_to_all | solution.py:111
  504.2 12.4 %gather_fusion.11 = f32[3072,14]{1,0:T(8,128)} fusion(f32[14,3072]{0,1:T(8,128)} %bitcast.427, s32[3072]{0:T(1024)S(1)} %copy-done.91), kind=kCustom, calls=%fused_computation.11 | custom fusion | bytes 356352 | tf_op jit(solution)/shard_map/gather | solution.py:118
  544.1 13.7 %fusion.64 = f32[48,64,256]{2,1,0:T(8,128)S(1)} fusion(f32[48,256,64]{1,2,0:T(8,128)S(1)} %copy-done.176, f32[48,64]{1,0:T(8,128)S(1)} %copy-done.157, f32[48,64]{1,0:T(8,128)S(1)} %get-tuple-element.185, f32[48,64]{1,0:T(8,128)S(1)} %copy-done.108, f32[48,64]{1,0:T(8,128)S(1)} %get-tuple-element.202, f32[48,64]{1,0:T(8,128)S(1)} %get-tuple-element.184, ...), kind=kOutput, calls=%fused_computation.133 | convolution fusion | flops 663752704 | bytes 6477824 | tf_op jit(solution)/shard_map/transpose(jvp(transpose(jvp(jk,bkp->bjp))))/dot_general | solution.py:91
  579.9 13.3 %fusion.66 = (f32[48,64]{1,0:T(8,128)S(1)}, f32[48,64]{1,0:T(8,128)S(1)}, f32[48,64]{1,0:T(8,128)S(1)}, f32[48,64]{1,0:T(8,128)S(1)}, f32[48,64]{1,0:T(8,128)S(1)}, /*index=5*/f32[48,64]{1,0:T(8,128)S(1)}) fusion(f32[48,64]{1,0:T(8,128)S(1)} %copy-done.86, f32[48,64]{1,0:T(8,128)S(1)} %copy-done.146, f32[256]{0:T(256)S(1)} %copy-done.168, ...), kind=kOutput, calls=%fused_computation.135 | convolution fusion | flops 651937792 | bytes 6502400 | tf_op jit(solution)/shard_map/transpose(jvp(jk,bkp->bjp))/dot_general | solution.py:91
  596.9 8.1 %gather_fusion.14 = f32[3072,14]{1,0:T(8,128)S(1)} fusion(f32[14,3072]{0,1:T(8,128)S(1)} %bitcast.430, s32[3072]{0:T(1024)S(1)} %copy-done.88), kind=kCustom, calls=%fused_computation.14 | custom fusion | bytes 356352 | tf_op jit(solution)/shard_map/gather | solution.py:121
  605.5 12.1 %all_to_all.33 = f32[14,32,96]{2,0,1:T(8,128)S(1)} all-to-all(f32[14,32,96]{2,0,1:T(8,128)S(1)} %copy.437), channel_id=1, replica_groups=mesh['cell'=8,'view'=4] {'cell','view'}, dimensions={1} | all-to-all | bytes 344064 | tf_op jit(solution)/shard_map/all_to_all | solution.py:114
  621.1 18.3 %scatter_custom_fusion.2 = f32[2048,14]{1,0:T(8,128)} fusion(s32[3072]{0:T(1024)} %reshape.2786, f32[3072,14]{1,0:T(8,128)} %copy.439, f32[]{:T(128)} %constant.25.clone.1), kind=kCustom, calls=%fused_computation.294 | custom fusion | flops 43008 | bytes 115200 | tf_op jit(solution)/shard_map/scatter-add | solution.py:123
  641.5 38.5 %psum.31 = f32[]{:T(128)} all-reduce(f32[]{:T(128)} %multiply_reduce_fusion.3), channel_id=1, replica_groups=mesh['cell'=8,'view'=4] {'cell','view'}, use_global_device_ids=true, to_apply=%region_30.31 | all-reduce | flops 1 | bytes 8 | tf_op jit(solution)/shard_map/psum | solution.py:162
  (566 shorter events, 204.3 us)
Async XLA Ops:
  12.1 17.7 %all-to-all-start = ((f32[14,32,96]{2,0,1:T(8,128)}), f32[14,32,96]{2,0,1:T(8,128)S(1)}, u32[]{:S(2)}, u32[]{:S(2)}) async-start(f32[14,32,96]{2,0,1:T(8,128)} %bitcast.2), calls=%async_computation | async-start | bytes 524288 | tf_op jit(solution)/shard_map/all_to_all | solution.py:111
  57.6 8.7 %collective-permute-start = (f32[48,256]{1,0:T(8,128)S(1)}, f32[48,256]{1,0:T(8,128)S(1)}, u32[]{:S(2)}, u32[]{:S(2)}) collective-permute-start(f32[48,256]{1,0:T(8,128)S(1)} %bitcast.471), channel_id=1, source_target_pairs={{0,3},{1,0},{2,1},{3,2},{4,7},{5,4},{6,5},{7,6},{8,11},{9,8},{10,9... | collective-permute-start | bytes 147464 | tf_op jit(solution)/shard_map/ppermute | solution.py:15
  69.7 16.3 %collective-permute-start.1 = (f32[48,256]{1,0:T(8,128)}, f32[48,256]{1,0:T(8,128)}, u32[]{:S(2)}, u32[]{:S(2)}) collective-permute-start(f32[48,256]{1,0:T(8,128)} %gather_fusion.3), channel_id=1, source_target_pairs={{0,1},{1,2},{2,3},{3,0},{4,5},{5,6},{6,7},{7,4},{8,9},{9,10},{10,1... | collective-permute-start | bytes 147464 | tf_op jit(solution)/shard_map/ppermute | solution.py:15
  75.9 27.6 %copy-start.56 = (f32[1,48,64]{2,1,0:T(8,128)}, f32[1,48,64]{2,1,0:T(8,128)S(1)}, u32[]{:S(2)}) copy-start(f32[1,48,64]{2,1,0:T(8,128)S(1)} %div.471) | copy-start | bytes 36868
  76.0 27.3 %copy-start.16 = (f32[1,48,64]{2,1,0:T(8,128)}, f32[1,48,64]{2,1,0:T(8,128)S(1)}, u32[]{:S(2)}) copy-start(f32[1,48,64]{2,1,0:T(8,128)S(1)} %exp.339) | copy-start | bytes 36868
  76.8 26.7 %copy-start.19 = (f32[1,48,64]{2,1,0:T(8,128)}, f32[1,48,64]{2,1,0:T(8,128)S(1)}, u32[]{:S(2)}) copy-start(f32[1,48,64]{2,1,0:T(8,128)S(1)} %exp.340) | copy-start | bytes 36868
  77.6 25.8 %copy-start.22 = (f32[1,48,64]{2,1,0:T(8,128)}, f32[1,48,64]{2,1,0:T(8,128)S(1)}, u32[]{:S(2)}) copy-start(f32[1,48,64]{2,1,0:T(8,128)S(1)} %exp.341) | copy-start | bytes 36868
  122.9 19.2 %all-to-all-start.1 = ((f32[14,32,96]{2,0,1:T(8,128)}), f32[14,32,96]{2,0,1:T(8,128)}, u32[]{:S(2)}, u32[]{:S(2)}) async-start(f32[14,32,96]{2,0,1:T(8,128)} %copy.413), calls=%async_computation.1 | async-start | bytes 524288 | tf_op jit(solution)/shard_map/all_to_all | solution.py:114
  183.9 33.4 %copy-start.90 = (s32[3072]{0:T(1024)S(1)}, s32[3072]{0:T(1024)}, u32[]{:S(2)}) copy-start(s32[3072]{0:T(1024)} %copy-done.89) | copy-start | bytes 36868
  198.6 39.7 %copy-start.54 = (f32[48,64]{1,0:T(8,128)S(1)}, f32[48,64]{1,0:T(8,128)}, u32[]{:S(2)}) copy-start(f32[48,64]{1,0:T(8,128)} %copy-done.53) | copy-start | bytes 36868
  198.6 41.8 %copy-start.70 = (f32[48,64]{1,0:T(8,128)S(1)}, f32[48,64]{1,0:T(8,128)}, u32[]{:S(2)}) copy-start(f32[48,64]{1,0:T(8,128)} %copy-done.68) | copy-start | bytes 36868
  198.6 41.8 %copy-start.76 = (f32[48,64]{1,0:T(8,128)S(1)}, f32[48,64]{1,0:T(8,128)}, u32[]{:S(2)}) copy-start(f32[48,64]{1,0:T(8,128)} %copy-done.74) | copy-start | bytes 36868
  214.7 26.3 %copy-start.95 = (f32[1,3072]{1,0:T(1,128)S(1)}, f32[1,3072]{1,0:T(1,128)}, u32[]{:S(2)}) copy-start(f32[1,3072]{1,0:T(1,128)} %get-tuple-element.154) | copy-start | bytes 36868
  214.7 37.1 %copy-start.82 = (f32[48,64]{1,0:T(8,128)S(1)}, f32[48,64]{1,0:T(8,128)}, u32[]{:S(2)}) copy-start(f32[48,64]{1,0:T(8,128)} %copy-done.80) | copy-start | bytes 36868
  229.5 25.7 %copy-start.63 = (f32[48,64]{1,0:T(8,128)S(1)}, f32[48,64]{1,0:T(8,128)}, u32[]{:S(2)}) copy-start(f32[48,64]{1,0:T(8,128)} %copy-done.62) | copy-start | bytes 36868
  278.4 5.1 collective-permute-start.2
  287.0 6.2 collective-permute-start.3
  472.2 32.0 %copy-start.91 = (s32[3072]{0:T(1024)S(1)}, s32[3072]{0:T(1024)}, u32[]{:S(2)}) copy-start(s32[3072]{0:T(1024)} %copy-done.89) | copy-start | bytes 36868
  486.9 39.3 %copy-start.96 = (f32[1,3072]{1,0:T(1,128)S(1)}, f32[1,3072]{1,0:T(1,128)}, u32[]{:S(2)}) copy-start(f32[1,3072]{1,0:T(1,128)} %get-tuple-element.154) | copy-start | bytes 36868
  486.9 39.3 %copy-start.97 = (f32[1,3072]{1,0:T(1,128)S(1)}, f32[1,3072]{1,0:T(1,128)}, u32[]{:S(2)}) copy-start(f32[1,3072]{1,0:T(1,128)} %get-tuple-element.156) | copy-start | bytes 36868
  501.6 38.7 %copy-start.84 = (f32[48,64]{1,0:T(8,128)S(1)}, f32[48,64]{1,0:T(8,128)}, u32[]{:S(2)}) copy-start(f32[48,64]{1,0:T(8,128)} %copy-done.80) | copy-start | bytes 36868
  516.6 27.1 %copy-start.55 = (f32[48,64]{1,0:T(8,128)S(1)}, f32[48,64]{1,0:T(8,128)}, u32[]{:S(2)}) copy-start(f32[48,64]{1,0:T(8,128)} %copy-done.53) | copy-start | bytes 36868
  516.6 27.1 %copy-start.9 = (f32[48,64]{1,0:T(8,128)S(1)}, f32[48,64]{1,0:T(8,128)}, u32[]{:S(2)}) copy-start(f32[48,64]{1,0:T(8,128)} %copy-done.7) | copy-start | bytes 36868
  516.6 27.1 %copy-start.12 = (f32[48,64]{1,0:T(8,128)S(1)}, f32[48,64]{1,0:T(8,128)}, u32[]{:S(2)}) copy-start(f32[48,64]{1,0:T(8,128)} %copy-done.10) | copy-start | bytes 36868
  516.6 27.1 %copy-start.15 = (f32[48,64]{1,0:T(8,128)S(1)}, f32[48,64]{1,0:T(8,128)}, u32[]{:S(2)}) copy-start(f32[48,64]{1,0:T(8,128)} %copy-done.13) | copy-start | bytes 36868
  516.6 27.1 %copy-start.61 = (f32[48,64]{1,0:T(8,128)S(1)}, f32[48,64]{1,0:T(8,128)}, u32[]{:S(2)}) copy-start(f32[48,64]{1,0:T(8,128)} %copy-done.59) | copy-start | bytes 36868
  516.6 27.1 %copy-start.64 = (f32[48,64]{1,0:T(8,128)S(1)}, f32[48,64]{1,0:T(8,128)}, u32[]{:S(2)}) copy-start(f32[48,64]{1,0:T(8,128)} %copy-done.62) | copy-start | bytes 36868
  564.8 5.3 collective-permute-start.4
  573.6 6.2 collective-permute-start.5
  605.0 34.3 %copy-start.1 = (f32[14,2048]{0,1:T(8,128)S(1)}, f32[14,2048]{0,1:T(8,128)}, u32[]{:S(2)}) copy-start(f32[14,2048]{0,1:T(8,128)} %multiply_add_fusion.7) | copy-start | bytes 344068
  605.5 75.7 %copy-start = (f32[2048,1,14]{2,1,0:T(1,128)S(1)}, f32[2048,1,14]{2,1,0:T(1,128)}, u32[]{:S(2)}) copy-start(f32[2048,1,14]{2,1,0:T(1,128)} %fusion.338) | copy-start | bytes 344068
  605.5 75.7 %copy-start.3 = (f32[14,2048]{0,1:T(8,128)S(1)}, f32[14,2048]{0,1:T(8,128)}, u32[]{:S(2)}) copy-start(f32[14,2048]{0,1:T(8,128)} %copy-done.2) | copy-start | bytes 344068
  (154 other events, 1042.8 us)
where the time goes:
time: 701 us; the launch traced here: 689 us
  local copies, waits for them, and re-layouts  215 us (31%)
  blocking collectives  173 us (25%)
  matrix products  160 us (23%)
  other arithmetic  105 us (15%)
  starting transfers between devices  22.1 us (3%)
  between operations  7.35 us (1%)
    psum x2, blocking collectives, global_inner(): return lax.psum(jnp.sum(first * second), ('cell', 'view'))  79.2 us
    dot_general x6, matrix products, render(): jnp.einsum('jk,bkp->bjp', earlier, log_keep, precision=lax.Precision.HIGH...  78.2 us
    all_to_all x4, blocking collectives, route(): lax.all_to_all(outgoing, ('cell', 'view'), split_axis=1, concat_axis=1, t...  55.7 us
    scatter-add x3, other arithmetic, collect(): jax.ops.segment_sum(returned.reshape(14, -1).T, send_ids.reshape(-1), num...  54.9 us
    gather x6, local copies, waits for them, and re-layouts, deliver(): received = route(values[:, send_ids], True)  38.6 us
    psum x1, blocking collectives, local(): lax.psum(jnp.sum(direction * normal_image), ('cell', 'view'))  38.5 us
    gather x6, local copies, waits for them, and re-layouts, deliver(): return received.reshape(14, -1)[:, entries].reshape(14, tiles_here, 64)  38.4 us
    dot_general x2, matrix products, apply_scaling(): jnp.einsum('ijg,jg->ig', preconditioner, vector, precision=lax.Precision....  35.2 us
  transfers between devices with their start and end apart: 8, of which 2 were waited for; matrix products, arithmetic and copies ran while one was open for 8% of the time, Pallas kernels for 0%

commit v1 on v0

--- a/solution.py
+++ b/solution.py
@@ -108,8 +108,14 @@
 
     def route(outgoing, forward):
         if forward:
-            return lax.all_to_all(
-                outgoing, ("cell", "view"), split_axis=1, concat_axis=1, tiled=True
+            return jnp.concatenate(
+                lax.all_to_all(
+                    jnp.stack(jnp.split(outgoing, lax.axis_size(("cell", "view")), axis=1), 0),
+                    axis_name=("cell", "view"),
+                    split_axis=0,
+                    concat_axis=0,
+                ),
+                1,
             )
         return lax.all_to_all(outgoing, ("cell", "view"), split_axis=1, concat_axis=1, tiled=True)
 

time: 701 us -> 729 us (1.040)
  local copies, waits for them, and re-layouts: 215 us -> 233 us
  starting transfers between devices: 22.1 us -> 33.5 us
    all_to_all x4 -> x2, blocking collectives: 55.7 us -> 24.9 us  [route(): lax.all_to_all(outgoing, ('cell', 'view'), split_axis=1, concat_axis=1, t...]
    all_to_all x0 -> x2, blocking collectives: none -> 29.3 us  [route(): lax.all_to_all(jnp.stack(jnp.split(outgoing, lax.axis_size(('cell', 'view...]
    unnamed x360 -> x459, local copies, waits for them, and re-layouts: 21.2 us -> 41.6 us
    ppermute x6, starting transfers between devices: 8.63 us -> 20 us  [shifted(): lax.ppermute(value, axis, [(i, (i + by) % devices) for i in range(devices)])]
    all_to_all x2 -> x1, starting transfers between devices: 13.5 us -> 6.16 us  [route(): lax.all_to_all(outgoing, ('cell', 'view'), split_axis=1, concat_axis=1, t...]
    all_to_all x0 -> x1, starting transfers between devices: none -> 7.33 us  [route(): lax.all_to_all(jnp.stack(jnp.split(outgoing, lax.axis_size(('cell', 'view...]
where the time goes in v1:
time: 729 us; the launch traced here: 717 us
  local copies, waits for them, and re-layouts  233 us (32%)
  blocking collectives  172 us (24%)
  matrix products  159 us (22%)
  other arithmetic  105 us (14%)
  starting transfers between devices  33.5 us (5%)
  between operations  7.95 us (1%)
    psum x2, blocking collectives, global_inner(): return lax.psum(jnp.sum(first * second), ('cell', 'view'))  79.3 us
    dot_general x6, matrix products, render(): jnp.einsum('jk,bkp->bjp', earlier, log_keep, precision=lax.Precision.HIGH...  76.8 us
    scatter-add x3, other arithmetic, collect(): jax.ops.segment_sum(returned.reshape(14, -1).T, send_ids.reshape(-1), num...  55.1 us
    unnamed x459, local copies, waits for them, and re-layouts  41.6 us
    gather x6, local copies, waits for them, and re-layouts, deliver(): return received.reshape(14, -1)[:, entries].reshape(14, tiles_here, 64)  39.8 us
    psum x1, blocking collectives, local(): lax.psum(jnp.sum(direction * normal_image), ('cell', 'view'))  38.5 us
    gather x6, local copies, waits for them, and re-layouts, deliver(): received = route(values[:, send_ids], True)  36.6 us
    dot_general x2, matrix products, apply_scaling(): jnp.einsum('ijg,jg->ig', preconditioner, vector, precision=lax.Precision....  35.2 us
  transfers between devices with their start and end apart: 8, of which 2 were waited for; matrix products, arithmetic and copies ran while one was open for 8% of the time, Pallas kernels for 0%

profile of v1, /device:TPU:0, one launch (start us, length us, event | category | flops | bytes accessed | tf_op | source)
XLA Modules:
  0.0 716.7 jit_solution(8774722237358631193)
XLA Ops:
  2.7 8.1 %gather_fusion = f32[3072,14]{1,0:T(8,128)S(1)} fusion(f32[14,2048]{0,1:T(8,128)S(1)} %copy.716, s32[3072]{0:T(1024)S(1)} %broadcast_clamp_fusion.1), kind=kCustom, calls=%fused_computation | custom fusion | bytes 356352 | tf_op jit(solution)/shard_map/gather | solution.py:123
  30.7 7.3 %all-to-all-start = ((f32[32,14,1,96]{3,2,1,0:T(1,128)}), f32[32,14,1,96]{3,2,1,0:T(1,128)S(1)}, u32[]{:S(2)}, u32[]{:S(2)}) async-start(f32[32,14,1,96]{3,2,1,0:T(1,128)} %constant_dynamic-update-slice_fusion), calls=%async_computation | async-start | bytes 458752 | tf_op jit(solution)/shard_map/all_to_all | solution.py:112
  41.5 5.8 sort.35
  49.1 8.1 %gather_fusion.1 = f32[3072,14]{1,0:T(8,128)S(1)} fusion(f32[14,3072]{0,1:T(8,128)S(1)} %bitcast.815, s32[3072]{0:T(1024)S(1)} %broadcast_clamp_fusion), kind=kCustom, calls=%fused_computation.1 | custom fusion | bytes 356352 | tf_op jit(solution)/shard_map/gather | solution.py:124
  64.5 10.2 %bitcast_multiply_fusion.8 = (f32[48,64,256]{2,1,0:T(8,128)S(1)}, f32[48,256,64]{1,2,0:T(8,128)}) fusion(f32[48,64]{1,0:T(8,128)S(1)} %get-tuple-element.226, f32[48,64]{1,0:T(8,128)S(1)} %broadcast_subtract_fusion, f32[256]{0:T(256)S(1)} %copy-done.166, f32[48,64]{1,0:T(8,128)S(1)} %get-tuple-element.225, f32[48,64]{1,0:T(8,128)S(1)} %broadcast_subtract_fusion.1, ...), kind=kOutput, calls=%fused_computation.206 | convolution fusion | flops 624431104 | bytes 6367232 | tf_op jit(solution)/shard_map/jvp(jk,bkp->bjp)/dot_general | solution.py:91
  88.4 11.6 %collective-permute-start.1 = (f32[48,256]{1,0:T(8,128)}, f32[48,256]{1,0:T(8,128)}, u32[]{:S(2)}, u32[]{:S(2)}) collective-permute-start(f32[48,256]{1,0:T(8,128)} %gather_fusion.3), channel_id=1, source_target_pairs={{0,1},{1,2},{2,3},{3,0},{4,5},{5,6},{6,7},{7,4},{8,9},{9,10},{10,1... | collective-permute-start | bytes 147464 | tf_op jit(solution)/shard_map/ppermute | solution.py:15
  119.6 13.4 %fusion.44 = (f32[48,64]{1,0:T(8,128)S(1)}, f32[48,64]{1,0:T(8,128)S(1)}, f32[48,64]{1,0:T(8,128)S(1)}, f32[48,64]{1,0:T(8,128)S(1)}, f32[48,64]{1,0:T(8,128)S(1)}, /*index=5*/f32[48,64]{1,0:T(8,128)S(1)}) fusion(f32[48,64]{1,0:T(8,128)S(1)} %copy-done.81, f32[48,64]{1,0:T(8,128)S(1)} %copy-done.145, f32[256]{0:T(256)S(1)} %copy-done.167, ...), kind=kOutput, calls=%fused_computation.113 | convolution fusion | flops 651937792 | bytes 6502400 | tf_op jit(solution)/shard_map/transpose(jvp(jk,bkp->bjp))/dot_general | solution.py:91
  136.9 13.2 %gather_fusion.4 = f32[3072,14]{1,0:T(8,128)} fusion(f32[14,3072]{0,1:T(8,128)} %bitcast.818, s32[3072]{0:T(1024)} %fusion.294), kind=kCustom, calls=%fused_computation.4 | custom fusion | bytes 356352 | tf_op jit(solution)/shard_map/gather | solution.py:127
  152.8 6.2 all-to-all-start.1
  159.6 12.3 %copy.760 = f32[14,14,2048]{0,1,2:T(8,128)} copy(f32[14,14,2048]{2,1,0:T(8,128)} %param.10) | data formatting | bytes 3211264 | tf_op args[3]
  176.4 18.2 %scatter_custom_fusion = f32[2048,14]{1,0:T(8,128)} fusion(s32[3072]{0:T(1024)} %reshape.2786, f32[3072,14]{1,0:T(8,128)} %copy.727, f32[]{:T(128)} %constant.25.clone.1), kind=kCustom, calls=%fused_computation.298 | custom fusion | flops 43008 | bytes 115200 | tf_op jit(solution)/shard_map/scatter-add | solution.py:129
  195.9 17.7 %fusion.338 = f32[2048,1,14]{2,1,0:T(1,128)} fusion(f32[14,2048,1]{0,2,1:T(1,128)S(1)} %bitcast.820, f32[14,14,2048]{0,1,2:T(8,128)} %copy.760), kind=kOutput, calls=%fused_computation.820 | convolution fusion | flops 4816896 | bytes 1835008 | tf_op jit(solution)/shard_map/ijg,jg->ig/dot_general | solution.py:142
  213.6 12.0 %gather_fusion.5 = f32[3072,14]{1,0:T(8,128)} fusion(f32[14,2048]{0,1:T(8,128)} %bitcast.806, s32[3072]{0:T(1024)S(1)} %broadcast_clamp_fusion.1), kind=kCustom, calls=%fused_computation.5 | custom fusion | bytes 356352 | tf_op jit(solution)/shard_map/gather | solution.py:123
  228.2 15.3 %all_to_all.30 = f32[32,14,1,96]{3,2,1,0:T(1,128)S(1)} all-to-all(f32[32,14,1,96]{3,2,1,0:T(1,128)S(1)} %constant_dynamic-update-slice_fusion.32), channel_id=1, replica_groups=mesh['cell'=8,'view'=4] {'cell','view'}, dimensions={0} | all-to-all | bytes 344064 | tf_op jit(solution)/shard_map/all_to_all | solution.py:112
  245.2 13.6 %gather_fusion.6 = f32[3072,14]{1,0:T(8,128)} fusion(f32[14,3072]{0,1:T(8,128)} %bitcast.816, s32[3072]{0:T(1024)} %copy-done.91), kind=kCustom, calls=%fused_computation.6 | custom fusion | bytes 356352 | tf_op jit(solution)/shard_map/gather | solution.py:124
  288.1 13.5 %fusion.53 = f32[48,64,256]{2,1,0:T(8,128)S(1)} fusion(f32[48,256,64]{1,2,0:T(8,128)S(1)} %copy-done.177, f32[48,64]{1,0:T(8,128)S(1)} %copy-done.161, f32[48,64]{1,0:T(8,128)S(1)} %get-tuple-element.191, f32[48,64]{1,0:T(8,128)S(1)} %copy-done.110, f32[48,64]{1,0:T(8,128)S(1)} %copy-done.163, f32[48,64]{1,0:T(8,128)S(1)} %get-tuple-element.190, ...), kind=kOutput, calls=%fused_computation.122 | convolution fusion | flops 663752704 | bytes 6477824 | tf_op jit(solution)/shard_map/transpose(jvp(transpose(jvp(jk,bkp->bjp))))/dot_general | solution.py:91
  324.4 13.2 %fusion.55 = (f32[48,64]{1,0:T(8,128)S(1)}, f32[48,64]{1,0:T(8,128)S(1)}, f32[48,64]{1,0:T(8,128)S(1)}, f32[48,64]{1,0:T(8,128)S(1)}, f32[48,64]{1,0:T(8,128)S(1)}, /*index=5*/f32[48,64]{1,0:T(8,128)S(1)}) fusion(f32[48,64]{1,0:T(8,128)S(1)} %copy-done.84, f32[48,64]{1,0:T(8,128)S(1)} %copy-done.147, f32[256]{0:T(256)S(1)} %copy-done.169, ...), kind=kOutput, calls=%fused_computation.124 | convolution fusion | flops 651937792 | bytes 6502400 | tf_op jit(solution)/shard_map/transpose(jvp(jk,bkp->bjp))/dot_general | solution.py:91
  344.1 13.2 %gather_fusion.9 = f32[3072,14]{1,0:T(8,128)} fusion(f32[14,3072]{0,1:T(8,128)} %bitcast.819, s32[3072]{0:T(1024)} %fusion.294), kind=kCustom, calls=%fused_computation.9 | custom fusion | bytes 356352 | tf_op jit(solution)/shard_map/gather | solution.py:127
  360.0 12.8 %all_to_all.31 = f32[14,32,96]{2,0,1:T(8,128)S(1)} all-to-all(f32[14,32,96]{2,0,1:T(8,128)} %copy.737), channel_id=1, replica_groups=mesh['cell'=8,'view'=4] {'cell','view'}, dimensions={1} | all-to-all | bytes 344064 | tf_op jit(solution)/shard_map/all_to_all | solution.py:120
  376.2 18.6 %scatter_custom_fusion.1 = f32[2048,14]{1,0:T(8,128)} fusion(s32[3072]{0:T(1024)} %reshape.2786, f32[3072,14]{1,0:T(8,128)} %copy.739, f32[]{:T(128)} %constant.25.clone.1), kind=kCustom, calls=%fused_computation.296 | custom fusion | flops 43008 | bytes 115200 | tf_op jit(solution)/shard_map/scatter-add | solution.py:129
  397.7 38.6 %all-reduce.51 = (f32[]{:T(128)}, f32[]{:T(128)}) all-reduce(f32[]{:T(128)} %get-tuple-element.37, f32[]{:T(128)} %get-tuple-element.36), channel_id=1, replica_groups=mesh['cell'=8,'view'=4] {'cell','view'}, use_global_device_ids=true, to_apply=%region_10.11 | all-reduce | flops 2 | bytes 16 | tf_op jit(solution)/shard_map/psum | solution.py:145
  439.7 17.4 %fusion.342 = f32[2048,1,14]{2,1,0:T(1,128)S(1)} fusion(f32[14,2048,1]{0,2,1:T(1,128)S(1)} %bitcast.811, f32[14,14,2048]{0,1,2:T(8,128)} %copy.760), kind=kOutput, calls=%fused_computation.824 | convolution fusion | flops 4816896 | bytes 1835008 | tf_op jit(solution)/shard_map/ijg,jg->ig/dot_general | solution.py:142
  459.0 40.6 %psum.30 = f32[]{:T(128)} all-reduce(f32[]{:T(128)} %multiply_reduce_fusion.4), channel_id=1, replica_groups=mesh['cell'=8,'view'=4] {'cell','view'}, use_global_device_ids=true, to_apply=%region_21.22 | all-reduce | flops 1 | bytes 8 | tf_op jit(solution)/shard_map/psum | solution.py:145
  503.5 12.1 %gather_fusion.10 = f32[3072,14]{1,0:T(8,128)} fusion(f32[14,2048]{0,1:T(8,128)} %multiply_add_fusion.7, s32[3072]{0:T(1024)S(1)} %broadcast_clamp_fusion.1), kind=kCustom, calls=%fused_computation.10 | custom fusion | bytes 356352 | tf_op jit(solution)/shard_map/gather | solution.py:123
  518.2 13.9 %all_to_all.32 = f32[32,14,1,96]{3,2,1,0:T(1,128)S(1)} all-to-all(f32[32,14,1,96]{3,2,1,0:T(1,128)S(1)} %constant_dynamic-update-slice_fusion.64), channel_id=1, replica_groups=mesh['cell'=8,'view'=4] {'cell','view'}, dimensions={0} | all-to-all | bytes 344064 | tf_op jit(solution)/shard_map/all_to_all | solution.py:112
  533.7 12.4 %gather_fusion.11 = f32[3072,14]{1,0:T(8,128)} fusion(f32[14,3072]{0,1:T(8,128)} %bitcast.814, s32[3072]{0:T(1024)S(1)} %copy-done.92), kind=kCustom, calls=%fused_computation.11 | custom fusion | bytes 356352 | tf_op jit(solution)/shard_map/gather | solution.py:124
  572.2 13.5 %fusion.64 = f32[48,64,256]{2,1,0:T(8,128)S(1)} fusion(f32[48,256,64]{1,2,0:T(8,128)S(1)} %copy-done.179, f32[48,64]{1,0:T(8,128)S(1)} %copy-done.160, f32[48,64]{1,0:T(8,128)S(1)} %get-tuple-element.187, f32[48,64]{1,0:T(8,128)S(1)} %copy-done.108, f32[48,64]{1,0:T(8,128)S(1)} %get-tuple-element.204, f32[48,64]{1,0:T(8,128)S(1)} %get-tuple-element.186, ...), kind=kOutput, calls=%fused_computation.133 | convolution fusion | flops 663752704 | bytes 6477824 | tf_op jit(solution)/shard_map/transpose(jvp(transpose(jvp(jk,bkp->bjp))))/dot_general | solution.py:91
  607.8 13.2 %fusion.66 = (f32[48,64]{1,0:T(8,128)S(1)}, f32[48,64]{1,0:T(8,128)S(1)}, f32[48,64]{1,0:T(8,128)S(1)}, f32[48,64]{1,0:T(8,128)S(1)}, f32[48,64]{1,0:T(8,128)S(1)}, /*index=5*/f32[48,64]{1,0:T(8,128)S(1)}) fusion(f32[48,64]{1,0:T(8,128)S(1)} %copy-done.87, f32[48,64]{1,0:T(8,128)S(1)} %copy-done.149, f32[256]{0:T(256)S(1)} %copy-done.171, ...), kind=kOutput, calls=%fused_computation.135 | convolution fusion | flops 651937792 | bytes 6502400 | tf_op jit(solution)/shard_map/transpose(jvp(jk,bkp->bjp))/dot_general | solution.py:91
  624.6 8.1 %gather_fusion.14 = f32[3072,14]{1,0:T(8,128)S(1)} fusion(f32[14,3072]{0,1:T(8,128)S(1)} %bitcast.817, s32[3072]{0:T(1024)S(1)} %copy-done.90), kind=kCustom, calls=%fused_computation.14 | custom fusion | bytes 356352 | tf_op jit(solution)/shard_map/gather | solution.py:127
  633.3 12.1 %all_to_all.33 = f32[14,32,96]{2,0,1:T(8,128)S(1)} all-to-all(f32[14,32,96]{2,0,1:T(8,128)S(1)} %copy.749), channel_id=1, replica_groups=mesh['cell'=8,'view'=4] {'cell','view'}, dimensions={1} | all-to-all | bytes 344064 | tf_op jit(solution)/shard_map/all_to_all | solution.py:120
  648.9 18.3 %scatter_custom_fusion.2 = f32[2048,14]{1,0:T(8,128)} fusion(s32[3072]{0:T(1024)} %reshape.2786, f32[3072,14]{1,0:T(8,128)} %copy.751, f32[]{:T(128)} %constant.25.clone.1), kind=kCustom, calls=%fused_computation.294 | custom fusion | flops 43008 | bytes 115200 | tf_op jit(solution)/shard_map/scatter-add | solution.py:129
  669.2 38.5 %psum.31 = f32[]{:T(128)} all-reduce(f32[]{:T(128)} %multiply_reduce_fusion.3), channel_id=1, replica_groups=mesh['cell'=8,'view'=4] {'cell','view'}, use_global_device_ids=true, to_apply=%region_30.31 | all-reduce | flops 1 | bytes 8 | tf_op jit(solution)/shard_map/psum | solution.py:168
  (668 shorter events, 225.6 us)
Async XLA Ops:
  0.6 37.9 %copy-start.104 = (s32[48,64]{1,0:T(8,128)S(1)}, s32[48,64]{1,0:T(8,128)}, u32[]{:S(2)}) copy-start(s32[48,64]{1,0:T(8,128)} %param.12) | copy-start | bytes 36868
  0.6 38.1 %copy-start.164 = (f32[2,48]{1,0:T(2,128)S(1)}, f32[2,48]{1,0:T(2,128)}, u32[]{:S(2)}) copy-start(f32[2,48]{1,0:T(2,128)} %param.8) | copy-start | bytes 1156
  0.7 38.2 %copy-start.165 = (s32[48]{0:T(128)S(1)}, s32[48]{0:T(128)}, u32[]{:S(2)}) copy-start(s32[48]{0:T(128)} %param.13) | copy-start | bytes 580
  30.7 17.7 %all-to-all-start = ((f32[32,14,1,96]{3,2,1,0:T(1,128)}), f32[32,14,1,96]{3,2,1,0:T(1,128)S(1)}, u32[]{:S(2)}, u32[]{:S(2)}) async-start(f32[32,14,1,96]{3,2,1,0:T(1,128)} %constant_dynamic-update-slice_fusion), calls=%async_computation | async-start | bytes 458752 | tf_op jit(solution)/shard_map/all_to_all | solution.py:112
  76.4 8.7 %collective-permute-start = (f32[48,256]{1,0:T(8,128)S(1)}, f32[48,256]{1,0:T(8,128)S(1)}, u32[]{:S(2)}, u32[]{:S(2)}) collective-permute-start(f32[48,256]{1,0:T(8,128)S(1)} %bitcast.955), channel_id=1, source_target_pairs={{0,3},{1,0},{2,1},{3,2},{4,7},{5,4},{6,5},{7,6},{8,11},{9,8},{10,9... | collective-permute-start | bytes 147464 | tf_op jit(solution)/shard_map/ppermute | solution.py:15
  88.4 27.3 %collective-permute-start.1 = (f32[48,256]{1,0:T(8,128)}, f32[48,256]{1,0:T(8,128)}, u32[]{:S(2)}, u32[]{:S(2)}) collective-permute-start(f32[48,256]{1,0:T(8,128)} %gather_fusion.3), channel_id=1, source_target_pairs={{0,1},{1,2},{2,3},{3,0},{4,5},{5,6},{6,7},{7,4},{8,9},{9,10},{10,1... | collective-permute-start | bytes 147464 | tf_op jit(solution)/shard_map/ppermute | solution.py:15
  105.8 27.6 %copy-start.55 = (f32[1,48,64]{2,1,0:T(8,128)}, f32[1,48,64]{2,1,0:T(8,128)S(1)}, u32[]{:S(2)}) copy-start(f32[1,48,64]{2,1,0:T(8,128)S(1)} %div.471) | copy-start | bytes 36868
  105.9 27.3 %copy-start.16 = (f32[1,48,64]{2,1,0:T(8,128)}, f32[1,48,64]{2,1,0:T(8,128)S(1)}, u32[]{:S(2)}) copy-start(f32[1,48,64]{2,1,0:T(8,128)S(1)} %exp.339) | copy-start | bytes 36868
  106.7 26.7 %copy-start.19 = (f32[1,48,64]{2,1,0:T(8,128)}, f32[1,48,64]{2,1,0:T(8,128)S(1)}, u32[]{:S(2)}) copy-start(f32[1,48,64]{2,1,0:T(8,128)S(1)} %exp.340) | copy-start | bytes 36868
  107.4 25.8 %copy-start.22 = (f32[1,48,64]{2,1,0:T(8,128)}, f32[1,48,64]{2,1,0:T(8,128)S(1)}, u32[]{:S(2)}) copy-start(f32[1,48,64]{2,1,0:T(8,128)S(1)} %exp.341) | copy-start | bytes 36868
  152.8 19.2 %all-to-all-start.1 = ((f32[14,32,96]{2,0,1:T(8,128)}), f32[14,32,96]{2,0,1:T(8,128)}, u32[]{:S(2)}, u32[]{:S(2)}) async-start(f32[14,32,96]{2,0,1:T(8,128)} %copy.725), calls=%async_computation.1 | async-start | bytes 524288 | tf_op jit(solution)/shard_map/all_to_all | solution.py:120
  245.2 39.2 %copy-start.82 = (f32[48,64]{1,0:T(8,128)S(1)}, f32[48,64]{1,0:T(8,128)}, u32[]{:S(2)}) copy-start(f32[48,64]{1,0:T(8,128)} %copy-done.80) | copy-start | bytes 36868
  258.8 28.9 %copy-start.8 = (f32[48,64]{1,0:T(8,128)S(1)}, f32[48,64]{1,0:T(8,128)}, u32[]{:S(2)}) copy-start(f32[48,64]{1,0:T(8,128)} %copy-done.7) | copy-start | bytes 36868
  258.8 28.9 %copy-start.11 = (f32[48,64]{1,0:T(8,128)S(1)}, f32[48,64]{1,0:T(8,128)}, u32[]{:S(2)}) copy-start(f32[48,64]{1,0:T(8,128)} %copy-done.10) | copy-start | bytes 36868
  258.8 28.9 %copy-start.14 = (f32[48,64]{1,0:T(8,128)S(1)}, f32[48,64]{1,0:T(8,128)}, u32[]{:S(2)}) copy-start(f32[48,64]{1,0:T(8,128)} %copy-done.13) | copy-start | bytes 36868
  258.8 28.9 %copy-start.59 = (f32[48,64]{1,0:T(8,128)S(1)}, f32[48,64]{1,0:T(8,128)}, u32[]{:S(2)}) copy-start(f32[48,64]{1,0:T(8,128)} %copy-done.58) | copy-start | bytes 36868
  258.8 28.9 %copy-start.62 = (f32[48,64]{1,0:T(8,128)S(1)}, f32[48,64]{1,0:T(8,128)}, u32[]{:S(2)}) copy-start(f32[48,64]{1,0:T(8,128)} %copy-done.61) | copy-start | bytes 36868
  309.4 5.2 collective-permute-start.2
  318.1 6.2 collective-permute-start.3
  503.5 30.2 %copy-start.92 = (s32[3072]{0:T(1024)S(1)}, s32[3072]{0:T(1024)}, u32[]{:S(2)}) copy-start(s32[3072]{0:T(1024)} %copy-done.91) | copy-start | bytes 36868
  518.2 36.7 %copy-start.96 = (f32[1,3072]{1,0:T(1,128)S(1)}, f32[1,3072]{1,0:T(1,128)}, u32[]{:S(2)}) copy-start(f32[1,3072]{1,0:T(1,128)} %get-tuple-element.156) | copy-start | bytes 36868
  533.7 34.7 %copy-start.85 = (f32[48,64]{1,0:T(8,128)S(1)}, f32[48,64]{1,0:T(8,128)}, u32[]{:S(2)}) copy-start(f32[48,64]{1,0:T(8,128)} %copy-done.80) | copy-start | bytes 36868
  546.1 25.7 %copy-start.9 = (f32[48,64]{1,0:T(8,128)S(1)}, f32[48,64]{1,0:T(8,128)}, u32[]{:S(2)}) copy-start(f32[48,64]{1,0:T(8,128)} %copy-done.7) | copy-start | bytes 36868
  546.1 25.7 %copy-start.12 = (f32[48,64]{1,0:T(8,128)S(1)}, f32[48,64]{1,0:T(8,128)}, u32[]{:S(2)}) copy-start(f32[48,64]{1,0:T(8,128)} %copy-done.10) | copy-start | bytes 36868
  546.1 25.7 %copy-start.15 = (f32[48,64]{1,0:T(8,128)S(1)}, f32[48,64]{1,0:T(8,128)}, u32[]{:S(2)}) copy-start(f32[48,64]{1,0:T(8,128)} %copy-done.13) | copy-start | bytes 36868
  546.1 25.7 %copy-start.60 = (f32[48,64]{1,0:T(8,128)S(1)}, f32[48,64]{1,0:T(8,128)}, u32[]{:S(2)}) copy-start(f32[48,64]{1,0:T(8,128)} %copy-done.58) | copy-start | bytes 36868
  546.1 25.7 %copy-start.63 = (f32[48,64]{1,0:T(8,128)S(1)}, f32[48,64]{1,0:T(8,128)}, u32[]{:S(2)}) copy-start(f32[48,64]{1,0:T(8,128)} %copy-done.61) | copy-start | bytes 36868
  592.7 5.2 collective-permute-start.4
  601.5 6.2 collective-permute-start.5
  632.8 34.3 %copy-start.1 = (f32[14,2048]{0,1:T(8,128)S(1)}, f32[14,2048]{0,1:T(8,128)}, u32[]{:S(2)}) copy-start(f32[14,2048]{0,1:T(8,128)} %multiply_add_fusion.7) | copy-start | bytes 344068
  633.3 75.8 %copy-start = (f32[2048,1,14]{2,1,0:T(1,128)S(1)}, f32[2048,1,14]{2,1,0:T(1,128)}, u32[]{:S(2)}) copy-start(f32[2048,1,14]{2,1,0:T(1,128)} %fusion.338) | copy-start | bytes 344068
  633.3 75.8 %copy-start.3 = (f32[14,2048]{0,1:T(8,128)S(1)}, f32[14,2048]{0,1:T(8,128)}, u32[]{:S(2)}) copy-start(f32[14,2048]{0,1:T(8,128)} %copy-done.2) | copy-start | bytes 344068
  (157 other events, 1055.7 us)
